TPU v7x, 32 devices: a whole 2x2x4 slice. The times are simulated.
32 devices in a mesh: doc: 8 (over y, x, core), head: 4 (over z).
Axes of the slice: x: 2, y: 2, z: 4, core: 2. Of those that a mesh axis runs over, the one named last changes fastest.
Arguments:
- queries: bfloat16 [2048, 2048], P(('doc', 'head')), may hold values from -6 to 6
- keys: bfloat16 [2048, 2048], P(('doc', 'head')), may hold values from -6 to 6
- values: bfloat16 [2048, 2048], P(('doc', 'head')), may hold values from -6 to 6
- log_decay: bfloat16 [2048, 2048], P(('doc', 'head')), may hold values from -1 to 0
- beta_logit: bfloat16 [2048, 16], P(('doc', 'head')), may hold values from -6 to 6
- block_owner: int32 [8, 16], replicated, may hold values from 0 to 7, as said below
- block_start: int32 [8, 16], replicated, may hold values from 0 to 1, as said below
- gain: float32 [2048], P('head'), may hold values from 0.25 to 1.75
Outputs:
- attended: bfloat16 [4096, 2048], P('doc', 'head')
Inputs may be any that keep to these rules, and one draw needn't show every extreme that they name: `block_owner`: every block of index d of doc goes to owner (d + k) mod 8 for some k from 0 to 3; the blocks of one index with one owner form one run; a document lies in one run; at most 8 blocks of one index go to one owner, and exactly 8 to some owner of every index. `block_start`: the first block of every run of block_owner is 1; a document has 1 to 8 blocks.
All inputs are finite; a program needn't handle non-finite values.
Results may differ from a plain program's by a relative error of at most 0.001.
Values may be sent and summed in bfloat16 or wider, within the bound.
A program may use at most 64 MiB of HBM per device.

v0:
```python
import functools

import jax
import jax.numpy as jnp
from jax import lax
from jax.experimental import pallas as pl
from jax.experimental.pallas import tpu as pltpu
from jax.sharding import PartitionSpec as P

WIDTH = 128
BLOCK = 16
TILE = 128
RUNS = 4
BASE = 8

MESH = pl.DeviceIdType.MESH
F32 = jnp.float32
BF16 = jnp.bfloat16
NN = (((1,), (0,)), ((), ()))
NT = (((1,), (1,)), ((), ()))
TN = (((0,), (0,)), ((), ()))


def split(x):
    high = x.astype(BF16)
    return high, (x - high.astype(F32)).astype(BF16)


def bdot(a, b, dims=NN):
    return lax.dot_general(a, b, dims, preferred_element_type=F32)


def dot3(a, b, dims=NN):
    a_high, a_low = split(a) if not isinstance(a, tuple) else a
    b_high, b_low = split(b) if not isinstance(b, tuple) else b
    ca, cb = dims[0][0][0], dims[0][1][0]
    left = jnp.concatenate([a_high, a_low, a_high], axis=ca)
    right = jnp.concatenate([b_high, b_high, b_low], axis=cb)
    return bdot(left, right, dims)


def lane_iota(shape):
    return lax.broadcasted_iota(jnp.int32, shape, 1)


def row_iota(shape):
    return lax.broadcasted_iota(jnp.int32, shape, 0)


def inverses(mats):
    shape = (TILE, TILE)
    row, col = row_iota(shape), lane_iota(shape)
    eye = (row == col).astype(F32)
    diag = row // BASE == col // BASE
    neg = [jnp.where(diag, -a, 0.0) for a in mats]
    power = [dot3(n, n) for n in neg]
    inv = [eye + n for n in neg]
    size = 2
    while size < BASE:
        last = size * 2 >= BASE
        if last:
            inv = [x + dot3(x, p) for x, p in zip(inv, power)]
        else:
            both = [dot3(jnp.concatenate([x, p], axis=0), p) for x, p in zip(inv, power)]
            inv = [x + b[:TILE] for x, b in zip(inv, both)]
            power = [b[TILE:] for b in both]
        size *= 2
    size = BASE
    while size < TILE:
        off = (row // (2 * size) == col // (2 * size)) & (row // size > col // size)
        parts = [split(x) for x in inv]
        mid = [dot3(jnp.where(off, a, 0.0), x) for a, x in zip(mats, parts)]
        inv = [x - dot3(p, m) for x, p, m in zip(inv, parts, mid)]
        size *= 2
    return inv


def kernel(
    nz, nd, q_ref, k_ref, v_ref, g_ref, b_ref, owner_ref, start_ref, gain_ref, out_ref,
    buf, bbuf, place, stage, segcol, masks,
    send_sem, recv_sem, bsend_sem, brecv_sem, osend_sem, orecv_sem,
):
    me = lax.axis_index("head")
    doc = lax.axis_index("doc")
    heads, _, rowtok, _ = buf.shape
    tok = q_ref.shape[0]
    nblk = rowtok // BLOCK
    cap = 2 * nblk // RUNS
    capt = cap * BLOCK
    tiles = rowtok // TILE
    refs = (q_ref, k_ref, v_ref, g_ref)

    barrier = pltpu.get_barrier_semaphore()
    count = 0
    for step in range(1, nz):
        pl.semaphore_signal(
            barrier, inc=1, device_id={"head": lax.rem(me + step, nz)}, device_id_type=MESH
        )
        count += 1
    peers = sorted({s % nd for s in range(1, RUNS)} | {(-s) % nd for s in range(1, RUNS)})
    for step in peers:
        pl.semaphore_signal(
            barrier, inc=1, device_id={"doc": lax.rem(doc + step, nd)}, device_id_type=MESH
        )
        count += 1
    pl.semaphore_wait(barrier, count)

    mine = pl.ds(pl.multiple_of(me * tok, tok), tok)

    def incoming(step, head, which):
        partner = lax.rem(me + step, nz)
        column = pl.ds(pl.multiple_of((partner * heads + head) * WIDTH, WIDTH), WIDTH)
        source = refs[which].at[:, column]
        target = buf.at[head, which, mine, :]
        if step == 0:
            return pltpu.make_async_copy(source, target, recv_sem.at[0, head, which])
        return pltpu.make_async_remote_copy(
            src_ref=source,
            dst_ref=target,
            send_sem=send_sem.at[step, head, which],
            recv_sem=recv_sem.at[step, head, which],
            device_id={"head": partner},
            device_id_type=MESH,
        )

    def incoming_beta(step):
        if step == 0:
            return pltpu.make_async_copy(b_ref, bbuf.at[me], brecv_sem.at[0])
        return pltpu.make_async_remote_copy(
            src_ref=b_ref,
            dst_ref=bbuf.at[me],
            send_sem=bsend_sem.at[step],
            recv_sem=brecv_sem.at[step],
            device_id={"head": lax.rem(me + step, nz)},
            device_id_type=MESH,
        )

    def outgoing(run, head):
        rows = pl.ds(run * capt, capt)
        return pltpu.make_async_remote_copy(
            src_ref=stage.at[head, rows, :],
            dst_ref=out_ref.at[rows, pl.ds(pl.multiple_of(head * WIDTH, WIDTH), WIDTH)],
            send_sem=osend_sem.at[run, head],
            recv_sem=orecv_sem.at[run, head],
            device_id={"doc": lax.rem(doc + run, nd)},
            device_id_type=MESH,
        )

    for step in range(nz):
        incoming_beta(step).start()
    for head in range(heads):
        for step in list(range(1, nz)) + [0]:
            for which in range(4):
                incoming(step, head, which).start()

    here = row_iota((nd, nblk)) == doc
    owner = jnp.sum(jnp.where(here, owner_ref[...], 0), axis=0, keepdims=True)
    start = jnp.sum(jnp.where(here, start_ref[...], 0), axis=0, keepdims=True)
    eye_b = row_iota((nblk, nblk)) == lane_iota((nblk, nblk))
    owner_col = jnp.sum(jnp.where(eye_b, owner, 0), axis=1, keepdims=True)
    earlier = row_iota((nblk, nblk)) < lane_iota((nblk, nblk))
    rank = jnp.sum(jnp.where(earlier & (owner_col == owner), 1, 0), axis=0, keepdims=True)
    ahead = owner - doc
    ahead = jnp.where(ahead < 0, ahead + nd, ahead)
    slot = (ahead * cap + rank).astype(F32).astype(BF16)
    token_block = lane_iota((nblk, rowtok)) // BLOCK
    expand = (row_iota((nblk, rowtok)) == token_block).astype(F32).astype(BF16)
    slot_tok = bdot(slot, expand).astype(jnp.int32) * BLOCK + lane_iota((1, rowtok)) % BLOCK
    place[...] = (row_iota((RUNS * capt, rowtok)) == slot_tok).astype(F32).astype(BF16)
    upto = (row_iota((nblk, rowtok)) <= token_block).astype(F32).astype(BF16)
    seg_row = bdot(start.astype(F32).astype(BF16), upto)
    seg_col = jnp.sum(
        jnp.where(
            lane_iota((rowtok, nblk)) <= row_iota((rowtok, nblk)) // BLOCK, start.astype(F32), 0.0
        ),
        axis=1,
        keepdims=True,
    )
    segcol[...] = jnp.broadcast_to(seg_col, (rowtok, WIDTH))
    shape = (TILE, TILE)
    for tile in range(tiles):
        lo = tile * TILE
        same = seg_col[lo : lo + TILE] == seg_row[:, lo : lo + TILE]
        masks[tile, 0] = (same & (row_iota(shape) > lane_iota(shape))).astype(F32)
        masks[tile, 1] = (same & (row_iota(shape) >= lane_iota(shape))).astype(F32)

    for step in range(nz):
        if step == 0:
            incoming_beta(0).wait()
        else:
            incoming_beta(step).wait_recv()

    def one_head(head, carry):
        for step in range(nz):
            for which in range(4):
                if step == 0:
                    incoming(0, head, which).wait()
                else:
                    incoming(step, head, which).wait_recv()
        braw = bbuf[...].astype(F32).reshape(rowtok, bbuf.shape[2])
        braw = jnp.sum(
            jnp.where(lane_iota(braw.shape) == me * heads + head, braw, 0.0), axis=1, keepdims=True
        )
        beta = jax.nn.sigmoid(braw)
        lower = (row_iota(shape) >= lane_iota(shape)).astype(F32).astype(BF16)
        amats, scores, qgs, kgs, kes, ems, vs = [], [], [], [], [], [], []
        for tile in range(tiles):
            rows = pl.ds(tile * TILE, TILE)
            query = buf[head, 0, rows, :].astype(F32)
            key = buf[head, 1, rows, :].astype(F32)
            vs.append(buf[head, 2, rows, :].astype(F32))
            query = (
                query
                * lax.rsqrt(jnp.sum(query * query, axis=-1, keepdims=True) + 1e-06)
                * WIDTH ** (-0.5)
            )
            key = key * lax.rsqrt(jnp.sum(key * key, axis=-1, keepdims=True) + 1e-06)
            cumul = bdot(lower, buf[head, 3, rows, :])
            half = 0.5 * cumul[TILE - 1 :, :]
            grow = jnp.exp(cumul - half)
            shrink = jnp.exp(half - cumul)
            ems.append(jnp.exp(half))
            qg, kg, ki = query * grow, key * grow, key * shrink
            both = dot3(jnp.concatenate([kg, qg], axis=0), ki, NT)
            b = beta[tile * TILE : (tile + 1) * TILE]
            amats.append(jnp.where(masks[tile, 0] > 0.0, both[:TILE], 0.0) * b)
            scores.append(jnp.where(masks[tile, 1] > 0.0, both[TILE:], 0.0))
            qgs.append(qg)
            kgs.append(kg)
            kes.append(ki)
        invs = inverses(amats)
        state = None
        outs = []
        for tile in range(tiles):
            lo = tile * TILE
            b = beta[lo : lo + TILE]
            seg = segcol[lo : lo + TILE, :]
            right = vs[tile]
            if tile > 0:
                first = (seg == segcol[lo - 1 : lo, :]).astype(F32) * ems[tile]
                both = dot3(
                    jnp.concatenate([kgs[tile] * first, qgs[tile] * first], axis=0), state
                )
                right = right - both[:TILE]
            update = split(dot3(invs[tile], b * right))
            result = dot3(scores[tile], update)
            if tile > 0:
                result = result + both[TILE:]
            if tile < tiles - 1:
                last = (seg == segcol[lo + TILE - 1 : lo + TILE, :]).astype(F32) * ems[tile]
                added = dot3(kes[tile] * last, update, TN)
                if tile > 0:
                    scale = ems[tile] * ems[tile] * (
                        segcol[lo + TILE - 1 : lo + TILE, :] == segcol[lo - 1 : lo, :]
                    ).astype(F32)
                    eye = row_iota(shape) == lane_iota(shape)
                    scale = jnp.sum(jnp.where(eye, scale, 0.0), axis=1, keepdims=True)
                    added = added + scale * state
                state = added
            norm = lax.rsqrt(jnp.mean(result * result, axis=-1, keepdims=True) + 1e-05)
            gain = gain_ref[:, pl.ds(pl.multiple_of(head * WIDTH, WIDTH), WIDTH)]
            outs.append((result * norm * gain).astype(BF16))
        placed = bdot(place[...], jnp.concatenate(outs, axis=0)).astype(BF16)
        stage[head] = placed
        for run in range(1, RUNS):
            outgoing(run, head).start()
        out_ref[0:capt, pl.ds(pl.multiple_of(head * WIDTH, WIDTH), WIDTH)] = placed[:capt]
        return carry

    lax.fori_loop(0, heads, one_head, 0)

    def finish(head, carry):
        for step in range(1, nz):
            for which in range(4):
                incoming(step, head, which).wait_send()
        for run in range(1, RUNS):
            outgoing(run, head).wait()
        return carry

    for step in range(1, nz):
        incoming_beta(step).wait_send()
    lax.fori_loop(0, heads, finish, 0)


def solution(mesh):
    nz, nd = mesh.shape["head"], mesh.shape["doc"]

    def local(queries, keys, values, log_decay, beta_logit, block_owner, block_start, gain):
        tok, channels = queries.shape
        heads = channels // WIDTH // nz
        rowtok = tok * nz
        slots = 2 * rowtok
        vmem = pl.BlockSpec(memory_space=pltpu.VMEM)
        return pl.pallas_call(
            functools.partial(kernel, nz, nd),
            out_shape=jax.ShapeDtypeStruct((slots, heads * WIDTH), BF16),
            in_specs=[vmem] * 8,
            out_specs=vmem,
            scratch_shapes=[
                pltpu.VMEM((heads, 4, rowtok, WIDTH), BF16),
                pltpu.VMEM((nz, tok, beta_logit.shape[1]), BF16),
                pltpu.VMEM((slots, rowtok), BF16),
                pltpu.VMEM((heads, slots, WIDTH), BF16),
                pltpu.VMEM((rowtok, WIDTH), F32),
                pltpu.VMEM((rowtok // TILE, 2, TILE, TILE), F32),
                pltpu.SemaphoreType.DMA((nz, heads, 4)),
                pltpu.SemaphoreType.DMA((nz, heads, 4)),
                pltpu.SemaphoreType.DMA((nz,)),
                pltpu.SemaphoreType.DMA((nz,)),
                pltpu.SemaphoreType.DMA((RUNS, heads)),
                pltpu.SemaphoreType.DMA((RUNS, heads)),
            ],
            compiler_params=pltpu.CompilerParams(
                collective_id=0, has_side_effects=True, vmem_limit_bytes=60 * 1024 * 1024
            ),
            name="delta",
        )(
            queries, keys, values, log_decay, beta_logit, block_owner, block_start,
            gain.reshape(1, -1),
        )

    return jax.shard_map(
        local,
        mesh=mesh,
        in_specs=(P(("doc", "head"), None),) * 5 + (P(), P(), P("head")),
        out_specs=P("doc", "head"),
        check_vma=False,
    )
```

profile of v0, /device:TPU:0, one launch (start us, length us, event | category | flops | bytes accessed | tf_op | source)
XLA Modules:
  0.0 44.9 jit_solution(5626832597657912557)
XLA Ops:
  0.0 1.4 %copy.9.b_ref = bf16[64,16]{1,0:T(8,128)(2,1)} copy(bf16[64,16]{0,1:T(8,128)(2,1)} %param.12) | data formatting | bytes 4096 | tf_op args[4]
  1.4 41.7 %delta.1 = bf16[512,512]{1,0:T(8,128)(2,1)} custom-call(bf16[64,2048]{1,0:T(8,128)(2,1)} %q_ref.1, bf16[64,2048]{1,0:T(8,128)(2,1)} %k_ref.1, bf16[64,2048]{1,0:T(8,128)(2,1)} %v_ref.1, bf16[64,2048]{1,0:T(8,128)(2,1)} %g_ref.1, bf16[64,16]{1,0:T(8,128)(2,1)} %copy.9.b_ref, s32[8,16]{1,0:T(8,128)} %owner_ref.1, s32[8,16]{1,0:T(8,128)} %start_ref.1, ...), custom_call_target="tpu_custom_call" | custom-call | tf_op jit(solution)/shard_map/delta/pallas_call | solution.py:294
  43.1 1.9 %copy.11 = bf16[512,512]{1,0:T(8,128)(2,1)} copy(bf16[512,512]{1,0:T(8,128)(2,1)} %delta.1) | data formatting | bytes 1048576
where the time goes:
time: 45.2 us; the launch traced here: 44.9 us
  Pallas kernels  41.7 us (92%)
  local copies, waits for them, and re-layouts  3.24 us (7%)
    pallas_call x1, Pallas kernels, local(): pl.pallas_call(functools.partial(kernel, nz, nd), out_shape=jax.ShapeDtyp...  41.7 us
    unnamed x2, local copies, waits for them, and re-layouts  3.24 us

commit v1 on v0

--- a/solution.py
+++ b/solution.py
@@ -11,7 +11,7 @@
 BLOCK = 16
 TILE = 128
 RUNS = 4
-BASE = 8
+BASE = 16
 
 MESH = pl.DeviceIdType.MESH
 F32 = jnp.float32
@@ -34,9 +34,13 @@
     a_high, a_low = split(a) if not isinstance(a, tuple) else a
     b_high, b_low = split(b) if not isinstance(b, tuple) else b
     ca, cb = dims[0][0][0], dims[0][1][0]
-    left = jnp.concatenate([a_high, a_low, a_high], axis=ca)
-    right = jnp.concatenate([b_high, b_high, b_low], axis=cb)
-    return bdot(left, right, dims)
+    left = jnp.concatenate([a_high, a_low], axis=ca)
+    free = 1 - cb
+    top = jnp.concatenate([b_high, b_low], axis=free)
+    bottom = jnp.concatenate([b_high, jnp.zeros_like(b_low)], axis=free)
+    both = bdot(left, jnp.concatenate([top, bottom], axis=cb), dims)
+    width = both.shape[1] // 2
+    return both[:, :width] + both[:, width:]
 
 
 def lane_iota(shape):
@@ -45,6 +49,21 @@
 
 def row_iota(shape):
     return lax.broadcasted_iota(jnp.int32, shape, 0)
+
+
+def neumann(neg, order, eye):
+    power = [dot3(n, n) for n in neg]
+    total = [eye + n for n in neg]
+    size = 2
+    while size < order:
+        if size * 2 >= order:
+            total = [x + dot3(x, p) for x, p in zip(total, power)]
+        else:
+            both = [dot3(jnp.concatenate([x, p], axis=0), p) for x, p in zip(total, power)]
+            total = [x + b[:TILE] for x, b in zip(total, both)]
+            power = [b[TILE:] for b in both]
+        size *= 2
+    return total
 
 
 def inverses(mats):
@@ -52,32 +71,16 @@
     row, col = row_iota(shape), lane_iota(shape)
     eye = (row == col).astype(F32)
     diag = row // BASE == col // BASE
-    neg = [jnp.where(diag, -a, 0.0) for a in mats]
-    power = [dot3(n, n) for n in neg]
-    inv = [eye + n for n in neg]
-    size = 2
-    while size < BASE:
-        last = size * 2 >= BASE
-        if last:
-            inv = [x + dot3(x, p) for x, p in zip(inv, power)]
-        else:
-            both = [dot3(jnp.concatenate([x, p], axis=0), p) for x, p in zip(inv, power)]
-            inv = [x + b[:TILE] for x, b in zip(inv, both)]
-            power = [b[TILE:] for b in both]
-        size *= 2
-    size = BASE
-    while size < TILE:
-        off = (row // (2 * size) == col // (2 * size)) & (row // size > col // size)
-        parts = [split(x) for x in inv]
-        mid = [dot3(jnp.where(off, a, 0.0), x) for a, x in zip(mats, parts)]
-        inv = [x - dot3(p, m) for x, p, m in zip(inv, parts, mid)]
-        size *= 2
-    return inv
+    inner = neumann([jnp.where(diag, -a, 0.0) for a in mats], BASE, eye)
+    parts = [split(x) for x in inner]
+    outer = [-dot3(p, jnp.where(diag, 0.0, a)) for p, a in zip(parts, mats)]
+    return [dot3(y, p) for y, p in zip(neumann(outer, TILE // BASE, eye), parts)]
 
 
 def kernel(
     nz, nd, q_ref, k_ref, v_ref, g_ref, b_ref, owner_ref, start_ref, gain_ref, out_ref,
-    buf, bbuf, place, stage, segcol, masks,
+    buf, bbuf, betas, place, stage, segcol, masks, growth, keyinv, keystate, keyend, halves,
+    inverse, update, states,
     send_sem, recv_sem, bsend_sem, brecv_sem, osend_sem, orecv_sem,
 ):
     me = lax.axis_index("head")
@@ -148,10 +151,11 @@
 
     for step in range(nz):
         incoming_beta(step).start()
-    for head in range(heads):
-        for step in list(range(1, nz)) + [0]:
-            for which in range(4):
-                incoming(step, head, which).start()
+    for group in ((1, 3), (2,), (0,)):
+        for head in range(heads):
+            for step in list(range(1, nz)) + [0]:
+                for which in group:
+                    incoming(step, head, which).start()
 
     here = row_iota((nd, nblk)) == doc
     owner = jnp.sum(jnp.where(here, owner_ref[...], 0), axis=0, keepdims=True)
@@ -190,75 +194,122 @@
         else:
             incoming_beta(step).wait_recv()
 
-    def one_head(head, carry):
-        for step in range(nz):
-            for which in range(4):
-                if step == 0:
-                    incoming(0, head, which).wait()
-                else:
-                    incoming(step, head, which).wait_recv()
-        braw = bbuf[...].astype(F32).reshape(rowtok, bbuf.shape[2])
-        braw = jnp.sum(
-            jnp.where(lane_iota(braw.shape) == me * heads + head, braw, 0.0), axis=1, keepdims=True
-        )
-        beta = jax.nn.sigmoid(braw)
+    eye_tok = (row_iota((tok, tok)) == lane_iota((tok, tok))).astype(F32).astype(BF16)
+    for step in range(nz):
+        turned = bdot(eye_tok, bbuf[step], NT)
+        betas[step * tok : (step + 1) * tok, :] = jax.nn.sigmoid(turned)
+
+    def arrive(head, which):
+        incoming(0, head, which).wait()
+        for step in range(1, nz):
+            incoming(step, head, which).wait_recv()
+
+    def beta_of(head):
+        values = betas[...]
+        mine_here = lane_iota(values.shape) == me * heads + head
+        return jnp.sum(jnp.where(mine_here, values, 0.0), axis=1, keepdims=True)
+
+    def before(tile):
+        return segcol[tile * TILE - 1 : tile * TILE, :]
+
+    def final(tile):
+        return segcol[(tile + 1) * TILE - 1 : (tile + 1) * TILE, :]
+
+    group = 2 if heads % 2 == 0 else 1
+
+    def keys_part(index, carry):
         lower = (row_iota(shape) >= lane_iota(shape)).astype(F32).astype(BF16)
-        amats, scores, qgs, kgs, kes, ems, vs = [], [], [], [], [], [], []
+        where, amats = [], []
+        for member in range(group):
+            head = index * group + member
+            arrive(head, 1)
+            arrive(head, 3)
+            beta = beta_of(head)
+            for tile in range(tiles):
+                rows = pl.ds(tile * TILE, TILE)
+                seg = segcol[rows, :]
+                key = buf[head, 1, rows, :].astype(F32)
+                key = key * lax.rsqrt(jnp.sum(key * key, axis=-1, keepdims=True) + 1e-06)
+                cumul = bdot(lower, buf[head, 3, rows, :])
+                half = 0.5 * cumul[TILE - 1 :, :]
+                grow = jnp.exp(cumul - half)
+                middle = jnp.exp(half)
+                kg, ki = key * grow, key * jnp.exp(half - cumul)
+                amat = dot3(kg, ki, NT)
+                amat = jnp.where(masks[tile, 0] > 0.0, amat, 0.0)
+                amats.append(amat * beta[tile * TILE : (tile + 1) * TILE])
+                where.append((head, rows))
+                growth[head, rows, :] = grow
+                keyinv[head, rows, :] = ki
+                halves[head, tile] = jnp.broadcast_to(middle, (8, WIDTH))
+                if tile > 0:
+                    keystate[head, rows, :] = kg * ((seg == before(tile)).astype(F32) * middle)
+                if tile < tiles - 1:
+                    keyend[head, rows, :] = ki * ((seg == final(tile)).astype(F32) * middle)
+        for (head, rows), inv in zip(where, inverses(amats)):
+            inverse[head, rows, :] = inv
+        return carry
+
+    lax.fori_loop(0, heads // group, keys_part, 0)
+
+    def values_part(index, carry):
+        members = [index * group + member for member in range(group)]
+        state = [None] * group
+        for head in members:
+            arrive(head, 2)
+        beta = [beta_of(head) for head in members]
+        for tile in range(tiles):
+            lo = tile * TILE
+            rows = pl.ds(lo, TILE)
+            right = [buf[head, 2, rows, :].astype(F32) for head in members]
+            if tile > 0:
+                right = [
+                    r - dot3(keystate[head, rows, :], s)
+                    for r, head, s in zip(right, members, state)
+                ]
+            new = [
+                dot3(inverse[head, rows, :], b[lo : lo + TILE] * r)
+                for head, b, r in zip(members, beta, right)
+            ]
+            for head, n in zip(members, new):
+                update[head, rows, :] = n
+            if tile < tiles - 1:
+                added = [dot3(keyend[head, rows, :], n, TN) for head, n in zip(members, new)]
+                if tile > 0:
+                    eye = row_iota(shape) == lane_iota(shape)
+                    unbroken = (final(tile) == before(tile)).astype(F32)
+                    for place_in, head in enumerate(members):
+                        middle = halves[head, tile, 0:1, :]
+                        scale = middle * middle * unbroken
+                        scale = jnp.sum(jnp.where(eye, scale, 0.0), axis=1, keepdims=True)
+                        added[place_in] = added[place_in] + scale * state[place_in]
+                state = added
+                for head, s in zip(members, state):
+                    states[head, tile] = s
+        return carry
+
+    lax.fori_loop(0, heads // group, values_part, 0)
+
+    def queries_part(head, carry):
+        arrive(head, 0)
+        gain = gain_ref[:, pl.ds(pl.multiple_of(head * WIDTH, WIDTH), WIDTH)]
+        outs = []
         for tile in range(tiles):
             rows = pl.ds(tile * TILE, TILE)
             query = buf[head, 0, rows, :].astype(F32)
-            key = buf[head, 1, rows, :].astype(F32)
-            vs.append(buf[head, 2, rows, :].astype(F32))
             query = (
                 query
                 * lax.rsqrt(jnp.sum(query * query, axis=-1, keepdims=True) + 1e-06)
                 * WIDTH ** (-0.5)
             )
-            key = key * lax.rsqrt(jnp.sum(key * key, axis=-1, keepdims=True) + 1e-06)
-            cumul = bdot(lower, buf[head, 3, rows, :])
-            half = 0.5 * cumul[TILE - 1 :, :]
-            grow = jnp.exp(cumul - half)
-            shrink = jnp.exp(half - cumul)
-            ems.append(jnp.exp(half))
-            qg, kg, ki = query * grow, key * grow, key * shrink
-            both = dot3(jnp.concatenate([kg, qg], axis=0), ki, NT)
-            b = beta[tile * TILE : (tile + 1) * TILE]
-            amats.append(jnp.where(masks[tile, 0] > 0.0, both[:TILE], 0.0) * b)
-            scores.append(jnp.where(masks[tile, 1] > 0.0, both[TILE:], 0.0))
-            qgs.append(qg)
-            kgs.append(kg)
-            kes.append(ki)
-        invs = inverses(amats)
-        state = None
-        outs = []
-        for tile in range(tiles):
-            lo = tile * TILE
-            b = beta[lo : lo + TILE]
-            seg = segcol[lo : lo + TILE, :]
-            right = vs[tile]
+            qg = query * growth[head, rows, :]
+            scores = dot3(qg, keyinv[head, rows, :], NT)
+            scores = jnp.where(masks[tile, 1] > 0.0, scores, 0.0)
+            result = dot3(scores, update[head, rows, :])
             if tile > 0:
-                first = (seg == segcol[lo - 1 : lo, :]).astype(F32) * ems[tile]
-                both = dot3(
-                    jnp.concatenate([kgs[tile] * first, qgs[tile] * first], axis=0), state
-                )
-                right = right - both[:TILE]
-            update = split(dot3(invs[tile], b * right))
-            result = dot3(scores[tile], update)
-            if tile > 0:
-                result = result + both[TILE:]
-            if tile < tiles - 1:
-                last = (seg == segcol[lo + TILE - 1 : lo + TILE, :]).astype(F32) * ems[tile]
-                added = dot3(kes[tile] * last, update, TN)
-                if tile > 0:
-                    scale = ems[tile] * ems[tile] * (
-                        segcol[lo + TILE - 1 : lo + TILE, :] == segcol[lo - 1 : lo, :]
-                    ).astype(F32)
-                    eye = row_iota(shape) == lane_iota(shape)
-                    scale = jnp.sum(jnp.where(eye, scale, 0.0), axis=1, keepdims=True)
-                    added = added + scale * state
-                state = added
+                first = (segcol[rows, :] == before(tile)).astype(F32) * halves[head, tile, 0:1, :]
+                result = result + dot3(qg * first, states[head, tile - 1])
             norm = lax.rsqrt(jnp.mean(result * result, axis=-1, keepdims=True) + 1e-05)
-            gain = gain_ref[:, pl.ds(pl.multiple_of(head * WIDTH, WIDTH), WIDTH)]
             outs.append((result * norm * gain).astype(BF16))
         placed = bdot(place[...], jnp.concatenate(outs, axis=0)).astype(BF16)
         stage[head] = placed
@@ -267,7 +318,7 @@
         out_ref[0:capt, pl.ds(pl.multiple_of(head * WIDTH, WIDTH), WIDTH)] = placed[:capt]
         return carry
 
-    lax.fori_loop(0, heads, one_head, 0)
+    lax.fori_loop(0, heads, queries_part, 0)
 
     def finish(head, carry):
         for step in range(1, nz):
@@ -293,16 +344,25 @@
         vmem = pl.BlockSpec(memory_space=pltpu.VMEM)
         return pl.pallas_call(
             functools.partial(kernel, nz, nd),
-            out_shape=jax.ShapeDtypeStruct((slots, heads * WIDTH), BF16),
-            in_specs=[vmem] * 8,
+            out_shape=pltpu.VMEM((slots, heads * WIDTH), BF16),
+            in_specs=[pl.BlockSpec(memory_space=pl.ANY)] * 4 + [vmem] * 4,
             out_specs=vmem,
             scratch_shapes=[
                 pltpu.VMEM((heads, 4, rowtok, WIDTH), BF16),
-                pltpu.VMEM((nz, tok, beta_logit.shape[1]), BF16),
+                pltpu.VMEM((nz, beta_logit.shape[1], tok), BF16),
+                pltpu.VMEM((rowtok, beta_logit.shape[1]), F32),
                 pltpu.VMEM((slots, rowtok), BF16),
                 pltpu.VMEM((heads, slots, WIDTH), BF16),
                 pltpu.VMEM((rowtok, WIDTH), F32),
                 pltpu.VMEM((rowtok // TILE, 2, TILE, TILE), F32),
+                pltpu.VMEM((heads, rowtok, WIDTH), F32),
+                pltpu.VMEM((heads, rowtok, WIDTH), F32),
+                pltpu.VMEM((heads, rowtok, WIDTH), F32),
+                pltpu.VMEM((heads, rowtok, WIDTH), F32),
+                pltpu.VMEM((heads, rowtok // TILE, 8, WIDTH), F32),
+                pltpu.VMEM((heads, rowtok, WIDTH), F32),
+                pltpu.VMEM((heads, rowtok, WIDTH), F32),
+                pltpu.VMEM((heads, rowtok // TILE, WIDTH, WIDTH), F32),
                 pltpu.SemaphoreType.DMA((nz, heads, 4)),
                 pltpu.SemaphoreType.DMA((nz, heads, 4)),
                 pltpu.SemaphoreType.DMA((nz,)),
@@ -315,7 +375,7 @@
             ),
             name="delta",
         )(
-            queries, keys, values, log_decay, beta_logit, block_owner, block_start,
+            queries, keys, values, log_decay, beta_logit.T, block_owner, block_start,
             gain.reshape(1, -1),
         )
 

time: 45.2 us -> 40.4 us (0.89)
  local copies, waits for them, and re-layouts: 3.24 us -> 0.8 us
  Pallas kernels: 41.7 us -> 39.4 us
    unnamed x2 -> x1, local copies, waits for them, and re-layouts: 3.24 us -> 0.8 us
    pallas_call x1, Pallas kernels: 41.7 us -> 39.4 us  [local(): pl.pallas_call(functools.partial(kernel, nz, nd), out_shape=pltpu.VMEM((s...]
where the time goes in v1:
time: 40.4 us; the launch traced here: 40.2 us
  Pallas kernels  39.4 us (98%)
  local copies, waits for them, and re-layouts  0.8 us (2%)
    pallas_call x1, Pallas kernels, local(): pl.pallas_call(functools.partial(kernel, nz, nd), out_shape=pltpu.VMEM((s...  39.4 us

profile of v1, /device:TPU:0, one launch (start us, length us, event | category | flops | bytes accessed | tf_op | source)
XLA Modules:
  0.0 40.2 jit_solution(4037006432241559355)
XLA Ops:
  0.0 39.4 %delta.1 = bf16[512,512]{1,0:T(8,128)(2,1)S(1)} custom-call(bf16[64,2048]{1,0:T(8,128)(2,1)} %q_ref.1, bf16[64,2048]{1,0:T(8,128)(2,1)} %k_ref.1, bf16[64,2048]{1,0:T(8,128)(2,1)} %v_ref.1, bf16[64,2048]{1,0:T(8,128)(2,1)} %g_ref.1, bf16[16,64]{1,0:T(8,128)(2,1)} %bitcast.2, s32[8,16]{1,0:T(8,128)} %owner_ref.1, s32[8,16]{1,0:T(8,128)} %start_ref.1, ...), custom_call_target="tpu_custom_call" | custom-call | tf_op jit(solution)/shard_map/delta/pallas_call | solution.py:345
  39.4 0.8 %copy.10 = bf16[512,512]{1,0:T(8,128)(2,1)} copy(bf16[512,512]{1,0:T(8,128)(2,1)S(1)} %delta.1) | data formatting | bytes 1048576

commit v2 on v1

--- a/solution.py
+++ b/solution.py
@@ -151,11 +151,13 @@
 
     for step in range(nz):
         incoming_beta(step).start()
-    for group in ((1, 3), (2,), (0,)):
-        for head in range(heads):
-            for step in list(range(1, nz)) + [0]:
-                for which in group:
-                    incoming(step, head, which).start()
+    early = max(heads - 2, 0)
+    order = [(head, which) for head in range(heads) for which in (1, 3)]
+    order += [(head, which) for head in range(early) for which in (2, 0)]
+    order += [(head, which) for which in (2, 0) for head in range(early, heads)]
+    for head, which in order:
+        for step in list(range(1, nz)) + [0]:
+            incoming(step, head, which).start()
 
     here = row_iota((nd, nblk)) == doc
     owner = jnp.sum(jnp.where(here, owner_ref[...], 0), axis=0, keepdims=True)
@@ -253,8 +255,8 @@
     lax.fori_loop(0, heads // group, keys_part, 0)
 
     def values_part(index, carry):
-        members = [index * group + member for member in range(group)]
-        state = [None] * group
+        members = [index]
+        state = [None]
         for head in members:
             arrive(head, 2)
         beta = [beta_of(head) for head in members]
@@ -288,7 +290,6 @@
                     states[head, tile] = s
         return carry
 
-    lax.fori_loop(0, heads // group, values_part, 0)
 
     def queries_part(head, carry):
         arrive(head, 0)
@@ -318,7 +319,12 @@
         out_ref[0:capt, pl.ds(pl.multiple_of(head * WIDTH, WIDTH), WIDTH)] = placed[:capt]
         return carry
 
-    lax.fori_loop(0, heads, queries_part, 0)
+    def both_parts(head, carry):
+        return queries_part(head, values_part(head, carry))
+
+    lax.fori_loop(0, early, both_parts, 0)
+    lax.fori_loop(early, heads, values_part, 0)
+    lax.fori_loop(early, heads, queries_part, 0)
 
     def finish(head, carry):
         for step in range(1, nz):

time: 40.4 us -> 39.7 us (0.983)
  Pallas kernels: 39.4 us -> 38.7 us
    pallas_call x1, Pallas kernels: 39.4 us -> 38.7 us  [local(): pl.pallas_call(functools.partial(kernel, nz, nd), out_shape=pltpu.VMEM((s...]
where the time goes in v2:
time: 39.7 us; the launch traced here: 39.5 us
  Pallas kernels  38.7 us (97%)
  local copies, waits for them, and re-layouts  0.8 us (2%)
    pallas_call x1, Pallas kernels, local(): pl.pallas_call(functools.partial(kernel, nz, nd), out_shape=pltpu.VMEM((s...  38.7 us
    unnamed x1, local copies, waits for them, and re-layouts  0.8 us

profile of v2, /device:TPU:0, one launch (start us, length us, event | category | flops | bytes accessed | tf_op | source)
XLA Modules:
  0.0 39.5 jit_solution(8116450107324159507)
XLA Ops:
  0.0 38.7 %delta.1 = bf16[512,512]{1,0:T(8,128)(2,1)S(1)} custom-call(bf16[64,2048]{1,0:T(8,128)(2,1)} %q_ref.1, bf16[64,2048]{1,0:T(8,128)(2,1)} %k_ref.1, bf16[64,2048]{1,0:T(8,128)(2,1)} %v_ref.1, bf16[64,2048]{1,0:T(8,128)(2,1)} %g_ref.1, bf16[16,64]{1,0:T(8,128)(2,1)} %bitcast.2, s32[8,16]{1,0:T(8,128)} %owner_ref.1, s32[8,16]{1,0:T(8,128)} %start_ref.1, ...), custom_call_target="tpu_custom_call" | custom-call | tf_op jit(solution)/shard_map/delta/pallas_call | solution.py:351
  38.7 0.8 %copy.10 = bf16[512,512]{1,0:T(8,128)(2,1)} copy(bf16[512,512]{1,0:T(8,128)(2,1)S(1)} %delta.1) | data formatting | bytes 1048576

commit v3 on v2

--- a/solution.py
+++ b/solution.py
@@ -314,7 +314,7 @@
             outs.append((result * norm * gain).astype(BF16))
         placed = bdot(place[...], jnp.concatenate(outs, axis=0)).astype(BF16)
         stage[head] = placed
-        for run in range(1, RUNS):
+        for run in range(RUNS - 1, 0, -1):
             outgoing(run, head).start()
         out_ref[0:capt, pl.ds(pl.multiple_of(head * WIDTH, WIDTH), WIDTH)] = placed[:capt]
         return carry

time: 39.7 us -> 40 us (level)
  no operation moved by 1% of the time
where the time goes in v3:
time: 40 us; the launch traced here: 39.8 us
  Pallas kernels  39 us (98%)
  local copies, waits for them, and re-layouts  0.8 us (2%)
    pallas_call x1, Pallas kernels, local(): pl.pallas_call(functools.partial(kernel, nz, nd), out_shape=pltpu.VMEM((s...  39 us

profile of v3, /device:TPU:0, one launch (start us, length us, event | category | flops | bytes accessed | tf_op | source)
XLA Modules:
  0.0 39.8 jit_solution(10036208530852125165)
XLA Ops:
  0.0 39.0 %delta.1 = bf16[512,512]{1,0:T(8,128)(2,1)S(1)} custom-call(bf16[64,2048]{1,0:T(8,128)(2,1)} %q_ref.1, bf16[64,2048]{1,0:T(8,128)(2,1)} %k_ref.1, bf16[64,2048]{1,0:T(8,128)(2,1)} %v_ref.1, bf16[64,2048]{1,0:T(8,128)(2,1)} %g_ref.1, bf16[16,64]{1,0:T(8,128)(2,1)} %bitcast.2, s32[8,16]{1,0:T(8,128)} %owner_ref.1, s32[8,16]{1,0:T(8,128)} %start_ref.1, ...), custom_call_target="tpu_custom_call" | custom-call | tf_op jit(solution)/shard_map/delta/pallas_call | solution.py:351
  39.0 0.8 %copy.10 = bf16[512,512]{1,0:T(8,128)(2,1)} copy(bf16[512,512]{1,0:T(8,128)(2,1)S(1)} %delta.1) | data formatting | bytes 1048576
